TPU v7x, 32 devices: a whole 2x2x4 slice. The times are simulated.
32 devices in a mesh: wide: 16 (over z, x, core), seq: 2 (over y).
Axes of the slice: x: 2, y: 2, z: 4, core: 2. Of those that a mesh axis runs over, the one named last changes fastest.
Arguments:
- latents: bfloat16 [208, 128, 1152], P('wide', 'seq'), may hold values from -6 to 6
- skip_store: bfloat16 [208, 128, 1152], P('wide', None, 'seq'), may hold values from -6 to 6
- lengths: int32 [208], P('wide'), may hold values from 80 to 128, as said below
- cotangent: bfloat16 [208, 128, 1152], P('wide', 'seq'), may hold values from -6 to 6
- skip_weight: bfloat16 [2304, 1152], P('seq'), may hold values from -0.125 to 0.125
- skip_bias: bfloat16 [1152], P('seq'), may hold values from -1.75 to 1.75
- first_gain: bfloat16 [1152], P('seq'), may hold values from 0.099609375 to 1.8984375
- first_shift: bfloat16 [1152], P('seq'), may hold values from -1.75 to 1.75
- inward_weight: bfloat16 [1152, 3456], P('seq'), may hold values from -0.1875 to 0.1875
- outward_weight: bfloat16 [1152, 1152], P('seq'), may hold values from -0.5 to 0.5
- outward_bias: bfloat16 [1152], P('seq'), may hold values from -1.75 to 1.75
- second_gain: bfloat16 [1152], P('seq'), may hold values from 0.099609375 to 1.8984375
- second_shift: bfloat16 [1152], P('seq'), may hold values from -1.75 to 1.75
- expand_weight: bfloat16 [1152, 4608], P('seq'), may hold values from -0.1875 to 0.1875
- expand_bias: bfloat16 [4608], P('seq'), may hold values from -1.75 to 1.75
- contract_weight: bfloat16 [4608, 1152], P('seq'), may hold values from -0.09375 to 0.09375
- contract_bias: bfloat16 [1152], P('seq'), may hold values from -1.75 to 1.75
Outputs:
- output: bfloat16 [208, 128, 1152], P('wide', 'seq')
- latents_grad: float32 [208, 128, 1152], P('wide', 'seq')
- skip_grad: bfloat16 [208, 128, 1152], P('wide', None, 'seq')
- skip_weight_grad: float32 [2304, 1152], P('seq')
- skip_bias_grad: float32 [1152], P('seq')
- first_gain_grad: float32 [1152], P('seq')
- first_shift_grad: float32 [1152], P('seq')
- inward_weight_grad: float32 [1152, 3456], P('seq')
- outward_weight_grad: float32 [1152, 1152], P('seq')
- outward_bias_grad: float32 [1152], P('seq')
- second_gain_grad: float32 [1152], P('seq')
- second_shift_grad: float32 [1152], P('seq')
- expand_weight_grad: float32 [1152, 4608], P('seq')
- expand_bias_grad: float32 [4608], P('seq')
- contract_weight_grad: float32 [4608, 1152], P('seq')
- contract_bias_grad: float32 [1152], P('seq')
Inputs may be any that keep to these rules, and one draw needn't show every extreme that they name: `lengths`: among the 13 items of each index of wide, at least one has all 128 slots live.
All inputs are finite; a program needn't handle non-finite values.
Results may differ from a plain program's by a relative error of at most 0.02.
Values may be sent and summed in bfloat16 or wider, within the bound.
No kernel may reach another device: no remote copies, remote signals or barrier semaphores. Data moves between devices by JAX's collectives and lax.ppermute only.
A program may use at most 512 MiB of HBM per device.

v0:
```python
import jax
import jax.numpy as jnp
from jax import lax
from jax.sharding import PartitionSpec as P

HEAD_DIM = 72
EPS = 1e-05
NEG = -1e30


def across(left_side, right_side):
    return lax.dot_general(
        left_side, right_side, (((0,), (0,)), ((), ())), preferred_element_type=jnp.float32
    )


def against(left_side, right_side):
    return lax.dot_general(
        left_side, right_side, (((1,), (1,)), ((), ())), preferred_element_type=jnp.float32
    )


def simple(left_side, right_side):
    return jnp.dot(left_side, right_side, preferred_element_type=jnp.float32)


def layer_norm(hidden, gain, shift):
    mean_val = jnp.mean(hidden, -1, keepdims=True)
    centred = hidden - mean_val
    var_val = jnp.mean(centred * centred, -1, keepdims=True)
    return centred * lax.rsqrt(var_val + EPS) * gain + shift


def exact_gelu(values_in):
    return jax.nn.gelu(values_in, approximate=False)


def masked_scores(queries, keys_all, key_valid, score_scale):
    scores = (
        jnp.einsum("iqhd,ikhd->ihqk", queries, keys_all, preferred_element_type=jnp.float32)
        * score_scale
    )
    return jnp.where(key_valid[:, None, None, :], scores, NEG)


def attend(queries, keys_all, values_all, key_valid, score_scale):
    scores = masked_scores(queries, keys_all, key_valid, score_scale)
    peak = jnp.max(scores, -1, keepdims=True)
    raised = jnp.exp(scores - peak)
    total = jnp.sum(raised, -1, keepdims=True)
    probs = (raised / total).astype(jnp.bfloat16)
    mixed = jnp.einsum("ihqk,ikhd->iqhd", probs, values_all, preferred_element_type=jnp.float32)
    return (mixed.astype(jnp.bfloat16), peak + jnp.log(total))


def attend_back(queries, keys_all, values_all, key_valid, score_scale, log_total, grad_mixed):
    scores = masked_scores(queries, keys_all, key_valid, score_scale)
    probs = jnp.exp(scores - log_total)
    grad_probs = jnp.einsum(
        "iqhd,ikhd->ihqk", grad_mixed, values_all, preferred_element_type=jnp.float32
    )
    grad_scores = probs * (grad_probs - jnp.sum(grad_probs * probs, -1, keepdims=True))
    grad_scores = grad_scores.astype(jnp.bfloat16)
    grad_query = (
        jnp.einsum("ihqk,ikhd->iqhd", grad_scores, keys_all, preferred_element_type=jnp.float32)
        * score_scale
    )
    grad_key = (
        jnp.einsum("ihqk,iqhd->ikhd", grad_scores, queries, preferred_element_type=jnp.float32)
        * score_scale
    )
    grad_value = jnp.einsum(
        "ihqk,iqhd->ikhd",
        probs.astype(jnp.bfloat16),
        grad_mixed,
        preferred_element_type=jnp.float32,
    )
    return (grad_query, grad_key, grad_value)


def per_device(
    latents,
    skip_store,
    lengths,
    cotangent,
    skip_weight,
    skip_bias,
    first_gain,
    first_shift,
    inward_weight,
    outward_weight,
    outward_bias,
    second_gain,
    second_shift,
    expand_weight,
    expand_bias,
    contract_weight,
    contract_bias,
):
    shards = (
        skip_weight,
        skip_bias,
        first_gain,
        first_shift,
        inward_weight,
        outward_weight,
        outward_bias,
        second_gain,
        second_shift,
        expand_weight,
        expand_bias,
        contract_weight,
        contract_bias,
    )
    (
        skip_matrix,
        skip_offset,
        gain_first,
        shift_first,
        inward_matrix,
        outward_matrix,
        outward_offset,
        gain_second,
        shift_second,
        expand_matrix,
        expand_offset,
        contract_matrix,
        contract_offset,
    ) = (
        lax.all_gather(shards[0], "seq", axis=0, tiled=True),
        lax.all_gather(shards[1], "seq", axis=0, tiled=True),
        lax.all_gather(shards[2], "seq", axis=0, tiled=True),
        lax.all_gather(shards[3], "seq", axis=0, tiled=True),
        lax.all_gather(shards[4], "seq", axis=0, tiled=True),
        lax.all_gather(shards[5], "seq", axis=0, tiled=True),
        lax.all_gather(shards[6], "seq", axis=0, tiled=True),
        lax.all_gather(shards[7], "seq", axis=0, tiled=True),
        lax.all_gather(shards[8], "seq", axis=0, tiled=True),
        lax.all_gather(shards[9], "seq", axis=0, tiled=True),
        lax.all_gather(shards[10], "seq", axis=0, tiled=True),
        lax.all_gather(shards[11], "seq", axis=0, tiled=True),
        lax.all_gather(shards[12], "seq", axis=0, tiled=True),
    )
    gain_first = gain_first.astype(jnp.float32)
    shift_first = shift_first.astype(jnp.float32)
    gain_second = gain_second.astype(jnp.float32)
    shift_second = shift_second.astype(jnp.float32)
    item_count, slot_dev, model_width = latents.shape
    row_count = item_count * slot_dev
    seq_ways = lax.axis_size("seq")
    slot_count = slot_dev * seq_ways
    head_width = HEAD_DIM
    head_count = model_width // head_width
    score_scale = head_width ** (-0.5)
    key_valid = jnp.arange(slot_count, dtype=jnp.int32)[None, :] < lengths[:, None]
    skip_rows = lax.all_to_all(skip_store, "seq", split_axis=1, concat_axis=2, tiled=True)
    joined = jnp.concatenate([latents, skip_rows], -1).reshape(row_count, 2 * model_width)
    base = simple(joined, skip_matrix) + skip_offset.astype(jnp.float32)
    first_normed = layer_norm(base, gain_first, shift_first).astype(jnp.bfloat16)
    qkv_vals = simple(first_normed, inward_matrix).astype(jnp.bfloat16)
    qkv_split = qkv_vals.reshape(item_count, slot_dev, 3, head_count, head_width)
    queries = qkv_split[:, :, 0]
    keys_all, values_all = (
        lax.all_gather(qkv_split[:, :, 1], "seq", axis=1, tiled=True),
        lax.all_gather(qkv_split[:, :, 2], "seq", axis=1, tiled=True),
    )
    mixed, log_total = attend(queries, keys_all, values_all, key_valid, score_scale)
    mixed_rows = mixed.reshape(row_count, model_width)
    middle = base + simple(mixed_rows, outward_matrix) + outward_offset.astype(jnp.float32)
    second_normed = layer_norm(middle, gain_second, shift_second).astype(jnp.bfloat16)
    upper = simple(second_normed, expand_matrix) + expand_offset.astype(jnp.float32)
    activated = exact_gelu(upper).astype(jnp.bfloat16)
    result = middle + simple(activated, contract_matrix) + contract_offset.astype(jnp.float32)
    output = result.astype(jnp.bfloat16).reshape(item_count, slot_dev, model_width)
    grad_out = cotangent.reshape(row_count, model_width)
    grad_result = grad_out.astype(jnp.float32)
    grad_contract = across(activated, grad_out)
    grad_contract_off = jnp.sum(grad_result, 0)
    grad_act = against(grad_out, contract_matrix)
    unused_value, gelu_back = jax.vjp(exact_gelu, upper)
    grad_upper = gelu_back(grad_act)[0].astype(jnp.bfloat16)
    grad_expand = across(second_normed, grad_upper)
    grad_expand_off = jnp.sum(grad_upper.astype(jnp.float32), 0)
    grad_second = against(grad_upper, expand_matrix)
    unused_norm, second_back = jax.vjp(layer_norm, middle, gain_second, shift_second)
    grad_mid_ln, grad_gain_two, grad_shift_two = second_back(grad_second)
    grad_middle = grad_result + grad_mid_ln
    grad_branch = grad_middle.astype(jnp.bfloat16)
    grad_outward = across(mixed_rows, grad_branch)
    grad_outward_off = jnp.sum(grad_branch.astype(jnp.float32), 0)
    grad_mixed = against(grad_branch, outward_matrix).astype(jnp.bfloat16)
    grad_heads = grad_mixed.reshape(item_count, slot_dev, head_count, head_width)
    grad_query, grad_key, grad_value = attend_back(
        queries, keys_all, values_all, key_valid, score_scale, log_total, grad_heads
    )
    key_local, value_local = (
        lax.psum_scatter(
            grad_key.astype(jnp.bfloat16), "seq", scatter_dimension=1, tiled=True
        ).astype(jnp.float32),
        lax.psum_scatter(
            grad_value.astype(jnp.bfloat16), "seq", scatter_dimension=1, tiled=True
        ).astype(jnp.float32),
    )
    grad_qkv = jnp.stack([grad_query, key_local, value_local], 2).astype(jnp.bfloat16)
    grad_qkv = grad_qkv.reshape(row_count, 3 * model_width)
    grad_inward = across(first_normed, grad_qkv)
    grad_first = against(grad_qkv, inward_matrix)
    unused_first, first_back = jax.vjp(layer_norm, base, gain_first, shift_first)
    grad_base_ln, grad_gain_one, grad_shift_one = first_back(grad_first)
    grad_base = (grad_middle + grad_base_ln).astype(jnp.bfloat16)
    grad_skipw = across(joined, grad_base)
    grad_skip_off = jnp.sum(grad_base.astype(jnp.float32), 0)
    grad_joined = against(grad_base, skip_matrix)
    grad_latents = grad_joined[:, :model_width].reshape(item_count, slot_dev, model_width)
    grad_skip_rows = (
        grad_joined[:, model_width:].astype(jnp.bfloat16).reshape(item_count, slot_dev, model_width)
    )
    grad_skip = lax.all_to_all(grad_skip_rows, "seq", split_axis=2, concat_axis=1, tiled=True)
    grad_terms = (
        grad_skipw,
        grad_skip_off,
        grad_gain_one,
        grad_shift_one,
        grad_inward,
        grad_outward,
        grad_outward_off,
        grad_gain_two,
        grad_shift_two,
        grad_expand,
        grad_expand_off,
        grad_contract,
        grad_contract_off,
    )
    grad_parts = (
        lax.psum_scatter(
            grad_terms[0].astype(jnp.bfloat16), "seq", scatter_dimension=0, tiled=True
        ).astype(jnp.float32),
        lax.psum_scatter(
            grad_terms[1].astype(jnp.bfloat16), "seq", scatter_dimension=0, tiled=True
        ).astype(jnp.float32),
        lax.psum_scatter(
            grad_terms[2].astype(jnp.bfloat16), "seq", scatter_dimension=0, tiled=True
        ).astype(jnp.float32),
        lax.psum_scatter(
            grad_terms[3].astype(jnp.bfloat16), "seq", scatter_dimension=0, tiled=True
        ).astype(jnp.float32),
        lax.psum_scatter(
            grad_terms[4].astype(jnp.bfloat16), "seq", scatter_dimension=0, tiled=True
        ).astype(jnp.float32),
        lax.psum_scatter(
            grad_terms[5].astype(jnp.bfloat16), "seq", scatter_dimension=0, tiled=True
        ).astype(jnp.float32),
        lax.psum_scatter(
            grad_terms[6].astype(jnp.bfloat16), "seq", scatter_dimension=0, tiled=True
        ).astype(jnp.float32),
        lax.psum_scatter(
            grad_terms[7].astype(jnp.bfloat16), "seq", scatter_dimension=0, tiled=True
        ).astype(jnp.float32),
        lax.psum_scatter(
            grad_terms[8].astype(jnp.bfloat16), "seq", scatter_dimension=0, tiled=True
        ).astype(jnp.float32),
        lax.psum_scatter(
            grad_terms[9].astype(jnp.bfloat16), "seq", scatter_dimension=0, tiled=True
        ).astype(jnp.float32),
        lax.psum_scatter(
            grad_terms[10].astype(jnp.bfloat16), "seq", scatter_dimension=0, tiled=True
        ).astype(jnp.float32),
        lax.psum_scatter(
            grad_terms[11].astype(jnp.bfloat16), "seq", scatter_dimension=0, tiled=True
        ).astype(jnp.float32),
        lax.psum_scatter(
            grad_terms[12].astype(jnp.bfloat16), "seq", scatter_dimension=0, tiled=True
        ).astype(jnp.float32),
    )
    (
        sum_skipw,
        sum_skipb,
        sum_gain1,
        sum_shift1,
        sum_inward,
        sum_outward,
        sum_outb,
        sum_gain2,
        sum_shift2,
        sum_expand,
        sum_expandb,
        sum_contract,
        sum_contractb,
    ) = (
        lax.psum(grad_parts[0].astype(jnp.bfloat16), "wide").astype(jnp.float32),
        lax.psum(grad_parts[1].astype(jnp.bfloat16), "wide").astype(jnp.float32),
        lax.psum(grad_parts[2].astype(jnp.bfloat16), "wide").astype(jnp.float32),
        lax.psum(grad_parts[3].astype(jnp.bfloat16), "wide").astype(jnp.float32),
        lax.psum(grad_parts[4].astype(jnp.bfloat16), "wide").astype(jnp.float32),
        lax.psum(grad_parts[5].astype(jnp.bfloat16), "wide").astype(jnp.float32),
        lax.psum(grad_parts[6].astype(jnp.bfloat16), "wide").astype(jnp.float32),
        lax.psum(grad_parts[7].astype(jnp.bfloat16), "wide").astype(jnp.float32),
        lax.psum(grad_parts[8].astype(jnp.bfloat16), "wide").astype(jnp.float32),
        lax.psum(grad_parts[9].astype(jnp.bfloat16), "wide").astype(jnp.float32),
        lax.psum(grad_parts[10].astype(jnp.bfloat16), "wide").astype(jnp.float32),
        lax.psum(grad_parts[11].astype(jnp.bfloat16), "wide").astype(jnp.float32),
        lax.psum(grad_parts[12].astype(jnp.bfloat16), "wide").astype(jnp.float32),
    )
    return (
        output,
        grad_latents,
        grad_skip,
        sum_skipw,
        sum_skipb,
        sum_gain1,
        sum_shift1,
        sum_inward,
        sum_outward,
        sum_outb,
        sum_gain2,
        sum_shift2,
        sum_expand,
        sum_expandb,
        sum_contract,
        sum_contractb,
    )


def solution(mesh):
    return jax.shard_map(
        per_device,
        mesh=mesh,
        in_specs=(
            P("wide", "seq", None),
            P("wide", None, "seq"),
            P("wide"),
            P("wide", "seq", None),
            P("seq", None),
            P("seq"),
            P("seq"),
            P("seq"),
            P("seq", None),
            P("seq", None),
            P("seq"),
            P("seq"),
            P("seq"),
            P("seq", None),
            P("seq"),
            P("seq", None),
            P("seq"),
        ),
        out_specs=(
            P("wide", "seq", None),
            P("wide", "seq", None),
            P("wide", None, "seq"),
            P("seq", None),
            P("seq"),
            P("seq"),
            P("seq"),
            P("seq", None),
            P("seq", None),
            P("seq"),
            P("seq"),
            P("seq"),
            P("seq", None),
            P("seq"),
            P("seq", None),
            P("seq"),
        ),
        check_vma=False,
    )
```

profile of v0, /device:TPU:0, one launch (start us, length us, event | category | flops | bytes accessed | tf_op | source)
XLA Modules:
  0.0 1866.0 jit_solution(10372359800916407453)
XLA Ops:
  8.8 5.2 copy.101
  13.9 4.2 all-to-all-start
  21.0 57.0 %all-reduce.18 = (bf16[1152]{0:T(1024)(128)(2,1)S(1)}, bf16[1152]{0:T(1024)(128)(2,1)S(1)}, bf16[1152]{0:T(1024)(128)(2,1)S(1)}, bf16[1152]{0:T(1024)(128)(2,1)S...) all-reduce(bf16[1152]{0:T(1024)(128)(2,1)S(1)} %dynamic-update-slic, ...), channel_id=1, replica_groups=mesh['wide'=16,'seq'=2] {'seq'}, use_global_device_ids=true, to_apply=%add | all-reduce | flops 6912 | bytes 27648
  81.6 4.5 concatenate.9
  86.1 21.3 %all-gather.11.cloned.1.call-done = bf16[2304,1152]{1,0:T(8,128)(2,1)} async-done(((bf16[1152,1152]{1,0:T(8,128)(2,1)}), bf16[2304,1152]{1,0:T(8,128)(2,1)}) %all-gather.11.cloned.1.call-update) | async-done | bytes 5308432 | tf_op jit(solution)/shard_map/all_gather | solution.py:130
  107.4 8.3 fusion.55
  118.8 89.9 %all-gather.13.cloned.1.call-done = bf16[1152,3456]{1,0:T(8,128)(2,1)} async-done(((bf16[576,3456]{1,0:T(8,128)(2,1)}), bf16[1152,3456]{1,0:T(8,128)(2,1)}) %all-gather.13.cloned.1.call-update) | async-done | bytes 7962640 | tf_op jit(solution)/shard_map/all_gather | solution.py:134
  208.8 13.9 convolution_convert_fusion.5
  222.7 21.1 %reshape.156 = bf16[13,64,3,16,72]{4,3,2,1,0:T(8,128)(2,1)} reshape(bf16[832,3456]{1,0:T(8,128)(2,1)} %convolution_convert_fusion.5) | data formatting | bytes 11501568 | tf_op jit(solution)/shard_map/reshape | solution.py:161
  243.8 6.3 fusion.53
  253.1 4.3 copy.125
  260.0 4.4 all-gather.2
  264.6 74.7 %all-gather.21.cloned.1.call-done = bf16[13,128,1,16,72]{4,3,2,0,1:T(8,128)(2,1)} async-done(((bf16[13,64,1,16,72]{4,3,2,0,1:T(8,128)(2,1)}), bf16[13,128,1,16,72]{4,3,2,0,1:T(8,128)(2,1)}) %all-gather.21.cloned.1.call-update) | async-done | bytes 3833872 | tf_op jit(solution)/shard_map/all_gather | solution.py:165
  339.3 9.7 copy.105
  349.0 78.6 %all-gather.23.cloned.1.call-done = bf16[13,128,1,16,72]{4,3,2,0,1:T(8,128)(2,1)} async-done(((bf16[13,64,1,16,72]{4,3,2,0,1:T(8,128)(2,1)}), bf16[13,128,1,16,72]{4,3,2,0,1:T(8,128)(2,1)}) %all-gather.23.cloned.1.call-update) | async-done | bytes 3833872 | tf_op jit(solution)/shard_map/all_gather | solution.py:164
  427.6 9.7 copy.108
  437.2 4.7 fusion.27
  446.5 5.1 convert_bitcast_fusion.1
  454.3 4.7 reshape.157
  459.0 9.4 all-gather.15.cloned.1.call-done
  468.4 6.5 fusion.56
  477.6 123.1 %all-gather.17.cloned.1.call-done = bf16[1152,4608]{1,0:T(8,128)(2,1)} async-done(((bf16[576,4608]{1,0:T(8,128)(2,1)}), bf16[1152,4608]{1,0:T(8,128)(2,1)}) %all-gather.17.cloned.1.call-update) | async-done | bytes 10616848 | tf_op jit(solution)/shard_map/all_gather | solution.py:139
  600.8 17.9 fusion.45
  618.7 114.6 %all-gather.19.cloned.1.call-done = bf16[4608,1152]{1,0:T(8,128)(2,1)} async-done(((bf16[2304,1152]{1,0:T(8,128)(2,1)}), bf16[4608,1152]{1,0:T(8,128)(2,1)}) %all-gather.19.cloned.1.call-update) | async-done | bytes 10616848 | tf_op jit(solution)/shard_map/all_gather | solution.py:141
  733.3 49.8 %fusion.46 = (bf16[4608]{0:T(1024)(128)(2,1)}, bf16[832,4608]{1,0:T(8,128)(2,1)}, f32[832,4608]{1,0:T(8,128)}) fusion(f32[832,4608]{1,0:T(8,128)} %fusion.45, f32[4608]{0:T(1024)S(1)} %reshape.188, bf16[832,1152]{1,0:T(8,128)(2,1)S(1)} %bitcast.93, bf16[4608,1152]{1,0:T(8,128)(2,1)} %all-gather.19.cloned.1.call-done), kind=kOutput, calls=%fused_computation.97 | convolution fusion | flops 9116905472 | bytes 50899968 | tf_op jit(solution)/shard_map/dot_general | solution.py:18
  783.1 14.2 multiply_reduce_fusion.1
  806.3 8.4 reshape.160
  814.7 7.4 multiply_reduce_fusion
  822.1 4.4 multiply_convert_fusion.3
  832.3 9.4 copy.111
  843.7 7.4 convert_bitcast_fusion
  851.1 9.4 copy.114
  860.6 7.1 convolution_convert_fusion.4
  868.2 6.2 fusion.22
  874.3 50.4 %reduce-scatter.8.cloned.1.call-done = bf16[13,64,16,72]{3,2,0,1:T(8,128)(2,1)} async-done(((bf16[13,128,16,72]{3,2,0,1:T(8,128)(2,1)}), bf16[13,64,16,72]{3,2,0,1:T(8,128)(2,1)}) %reduce-scatter.8.cloned.1.call-update) | async-done | bytes 1916944 | tf_op jit(solution)/shard_map/reduce_scatter | solution.py:197
  927.6 82.9 %reduce-scatter.10.cloned.1.call-done = bf16[13,64,16,72]{3,2,0,1:T(8,128)(2,1)} async-done(((bf16[13,128,16,72]{3,2,0,1:T(8,128)(2,1)}), bf16[13,64,16,72]{3,2,0,1:T(8,128)(2,1)}) %reduce-scatter.10.cloned.1.call-update) | async-done | bytes 1916944 | tf_op jit(solution)/shard_map/reduce_scatter | solution.py:200
  1010.5 4.7 copy.141
  1015.1 9.5 pad_maximum_fusion
  1024.6 16.2 copy.116
  1040.8 16.7 convert_element_type.214
  1057.6 14.3 multiply_reduce_fusion.2
  1077.0 8.0 convolution_convert_fusion.3
  1085.7 17.8 convolution_convert_fusion.1
  1103.5 10.9 multiply_convert_fusion
  1117.4 14.4 convolution_convert_fusion
  1132.5 14.7 convolution_convert_fusion.2
  1147.4 4.2 reduce-scatter.12.cloned.1.call-done
  1151.5 126.1 %reduce-scatter.18.cloned.1.call-done = bf16[576,4608]{1,0:T(8,128)(2,1)} async-done(((bf16[1152,4608]{1,0:T(8,128)(2,1)}), bf16[576,4608]{1,0:T(8,128)(2,1)}) %reduce-scatter.18.cloned.1.call-update) | async-done | bytes 5308432 | tf_op jit(solution)/shard_map/reduce_scatter | solution.py:262
  1277.6 126.3 %reduce-scatter.20.cloned.1.call-done = bf16[2304,1152]{1,0:T(8,128)(2,1)} async-done(((bf16[4608,1152]{1,0:T(8,128)(2,1)}), bf16[2304,1152]{1,0:T(8,128)(2,1)}) %reduce-scatter.20.cloned.1.call-update) | async-done | bytes 5308432 | tf_op jit(solution)/shard_map/reduce_scatter | solution.py:268
  1403.9 97.4 %reduce-scatter.14.cloned.1.call-done = bf16[576,3456]{1,0:T(8,128)(2,1)} async-done(((bf16[1152,3456]{1,0:T(8,128)(2,1)}), bf16[576,3456]{1,0:T(8,128)(2,1)}) %reduce-scatter.14.cloned.1.call-update) | async-done | bytes 3981328 | tf_op jit(solution)/shard_map/reduce_scatter | solution.py:247
  1503.4 7.4 all-reduce.17
  1510.8 9.4 fusion.57
  1523.6 5.5 copy.117
  1529.1 5.3 reshape.212
  1538.2 17.4 fusion.19
  1555.5 4.3 slice.24
  1560.4 61.8 %all-reduce.15 = (bf16[576]{0:T(1024)(128)(2,1)S(1)}, bf16[576]{0:T(1024)(128)(2,1)S(1)}, bf16[576]{0:T(1024)(128)(2,1)S(1)}, bf16[576]{0:T(1024)(128)(2,1)S(1)}...) all-reduce(bf16[576]{0:T(1024)(128)(2,1)S(1)} %dynamic-slice.8, ...), channel_id=1, replica_groups=mesh['wide'=16,'seq'=2] {'wide'}, use_global_device_ids=true, to_apply=%region_17.18 | all-reduce | flops 6336 | bytes 25344 | tf_op jit(solution)/shard_map/psum | solution.py:291
  1627.0 4.4 reshape.213
  1631.4 9.2 copy.122
  1645.3 191.3 %all-reduce.21.cloned.1.call-done = (bf16[1152,1152]{1,0:T(8,128)(2,1)}, bf16[576,3456]{1,0:T(8,128)(2,1)}, bf16[576,1152]{1,0:T(8,128)(2,1)}, bf16[576,4608]{1,0:T(8,128)(2,1)}, bf16[2304,1152]{1,0:T(8,128)(2,1)}) async-done(((bf16[1152,1152]{1,0:T(8,128)(2,1)}, bf16[576,3456]{1,0:T(8,128)(2,1)}, bf16[576,1152]{1,0:T(8,128)(2,1)}, bf16[576,4608]{1,0:T(8,128)(2,1)}, bf16[2304,1152]{1,0:T(8,128)(2,1)}), ...) | async-done | bytes 18579472 | tf_op jit(solution)/shard_map/psum | solution.py:290
  1836.6 4.6 convert_element_type.217
  1844.3 4.6 convert_element_type.224
  1848.9 5.6 convert_element_type.233
  1854.5 4.8 convert_element_type.236
  (252 shorter events, 76.4 us)
Async XLA Ops:
  7.2 100.2 %all-gather.11.cloned.1.call-start = ((), (), s32[]{:S(2)}) async-start(), calls=%async_computation.9 | async-start | bytes 7962624 | tf_op jit(solution)/shard_map/all_gather | solution.py:130
  7.9 200.8 %all-gather.13.cloned.1.call-start = ((), (), s32[]{:S(2)}) async-start(), calls=%async_computation.10 | async-start | bytes 11943936 | tf_op jit(solution)/shard_map/all_gather | solution.py:134
  8.7 9.5 copy-start.55
  8.7 10.8 copy-start.56
  8.7 11.0 copy-start.57
  8.7 11.3 copy-start.58
  8.7 11.5 copy-start.59
  8.7 11.8 copy-start.60
  8.7 12.0 copy-start.61
  13.9 64.1 %all-to-all-start = ((bf16[13,128,576]{2,0,1:T(8,128)(2,1)}), bf16[13,128,576]{2,0,1:T(8,128)(2,1)S(1)}, u32[]{:S(2)}, u32[]{:S(2)}) async-start(bf16[13,128,576]{2,0,1:T(8,128)(2,1)} %copy.101), calls=%async_computation | async-start | bytes 5242880 | tf_op jit(solution)/shard_map/all_to_all | solution.py:156
  18.2 321.1 %all-gather.21.cloned.1.call-start = ((), (), s32[]{:S(2)}) async-start(), calls=%async_computation.21 | async-start | bytes 10223616 | tf_op jit(solution)/shard_map/all_gather | solution.py:165
  78.0 130.8 %copy-start.37 = (f32[1152]{0:T(1024)}, f32[1152]{0:T(1024)S(1)}, u32[]{:S(2)}) copy-start(f32[1152]{0:T(1024)S(1)} %convert_element_type.189) | copy-start | bytes 13828
  78.0 130.8 %copy-start.48 = (f32[1152]{0:T(1024)}, f32[1152]{0:T(1024)S(1)}, u32[]{:S(2)}) copy-start(f32[1152]{0:T(1024)S(1)} %convert_element_type.190) | copy-start | bytes 13828
  86.1 29.6 %copy-start.20 = (bf16[832,1152]{1,0:T(8,128)(2,1)}, bf16[832,1152]{1,0:T(8,128)(2,1)S(1)}, u32[]{:S(2)}) copy-start(bf16[832,1152]{1,0:T(8,128)(2,1)S(1)} %concatenate.9) | copy-start | bytes 5750788
  115.7 106.9 %copy-start.29 = (f32[832]{0:T(1024)}, f32[832]{0:T(1024)S(1)}, u32[]{:S(2)}) copy-start(f32[832]{0:T(1024)S(1)} %broadcast_multiply_fusion.1) | copy-start | bytes 9988
  118.8 103.8 %copy-start.41 = (f32[832]{0:T(1024)}, f32[832]{0:T(1024)S(1)}, u32[]{:S(2)}) copy-start(f32[832]{0:T(1024)S(1)} %fusion.37) | copy-start | bytes 9988
  250.1 187.1 %copy-start.3 = (bf16[13,64,1,16,72]{4,3,2,1,0:T(8,128)(2,1)}, bf16[13,64,1,16,72]{4,3,2,1,0:T(8,128)(2,1)S(1)}, u32[]{:S(2)}) copy-start(bf16[13,64,1,16,72]{4,3,2,1,0:T(8,128)(2,1)S(1)} %get-tuple-element.143) | copy-start | bytes 5750788
  252.8 174.7 %all-gather.23.cloned.1.call-start = ((), (), s32[]{:S(2)}) async-start(), calls=%async_computation.22 | async-start | bytes 10223616 | tf_op jit(solution)/shard_map/all_gather | solution.py:164
  257.4 211.0 %all-gather.15.cloned.1.call-start = ((), (), s32[]{:S(2)}) async-start(), calls=%async_computation.11 | async-start | bytes 3981312 | tf_op jit(solution)/shard_map/all_gather | solution.py:135
  258.0 342.8 %all-gather.17.cloned.1.call-start = ((), (), s32[]{:S(2)}) async-start(), calls=%async_computation.12 | async-start | bytes 15925248 | tf_op jit(solution)/shard_map/all_gather | solution.py:139
  258.6 5.9 copy-start.63
  258.6 474.7 %all-gather.19.cloned.1.call-start = ((), (), s32[]{:S(2)}) async-start(), calls=%async_computation.13 | async-start | bytes 15925248 | tf_op jit(solution)/shard_map/all_gather | solution.py:141
  259.3 665.4 %reduce-scatter.8.cloned.1.call-start = ((), (), s32[]{:S(2)}) async-start(), calls=%async_computation.14 | async-start | bytes 10223616 | tf_op jit(solution)/shard_map/reduce_scatter | solution.py:197
  259.4 341.4 %copy-start.39 = (f32[1152]{0:T(1024)}, f32[1152]{0:T(1024)S(1)}, u32[]{:S(2)}) copy-start(f32[1152]{0:T(1024)S(1)} %convert_element_type.197) | copy-start | bytes 13828
  259.4 341.4 %copy-start.50 = (f32[1152]{0:T(1024)}, f32[1152]{0:T(1024)S(1)}, u32[]{:S(2)}) copy-start(f32[1152]{0:T(1024)S(1)} %convert_element_type.198) | copy-start | bytes 13828
  264.6 181.4 %copy-start.27 = (pred[13,128]{1,0:T(8,128)(4,1)}, pred[13,128]{1,0:T(8,128)(4,1)S(1)}, u32[]{:S(2)}) copy-start(pred[13,128]{1,0:T(8,128)(4,1)S(1)} %iota_compare_fusion) | copy-start | bytes 4996
  441.9 9.7 copy-start
  441.9 4.5 copy-start.9
  446.5 5.2 copy-start.25
  474.9 143.8 %copy-start.31 = (f32[832]{0:T(1024)}, f32[832]{0:T(1024)S(1)}, u32[]{:S(2)}) copy-start(f32[832]{0:T(1024)S(1)} %broadcast_multiply_fusion) | copy-start | bytes 9988
  477.0 141.7 %copy-start.43 = (f32[832]{0:T(1024)}, f32[832]{0:T(1024)S(1)}, u32[]{:S(2)}) copy-start(f32[832]{0:T(1024)S(1)} %fusion.38) | copy-start | bytes 9988
  477.6 255.7 %copy-start.7 = (bf16[13,64,1152]{2,1,0:T(8,128)(2,1)S(1)}, bf16[13,64,1152]{2,1,0:T(8,128)(2,1)}, u32[]{:S(2)}) copy-start(bf16[13,64,1152]{2,1,0:T(8,128)(2,1)} %param.20) | copy-start | bytes 5750788
  733.3 49.8 %copy-start.13 = (f32[832,1152]{1,0:T(8,128)S(1)}, f32[832,1152]{1,0:T(8,128)}, u32[]{:S(2)}) copy-start(f32[832,1152]{1,0:T(8,128)} %copy-done.12) | copy-start | bytes 11501572
  733.3 49.8 %copy-start.32 = (f32[832]{0:T(1024)S(1)}, f32[832]{0:T(1024)}, u32[]{:S(2)}) copy-start(f32[832]{0:T(1024)} %copy-done.31) | copy-start | bytes 9988
  733.3 49.8 %copy-start.40 = (f32[1152]{0:T(1024)S(1)}, f32[1152]{0:T(1024)}, u32[]{:S(2)}) copy-start(f32[1152]{0:T(1024)} %copy-done.39) | copy-start | bytes 13828
  733.3 49.8 %copy-start.44 = (f32[832]{0:T(1024)S(1)}, f32[832]{0:T(1024)}, u32[]{:S(2)}) copy-start(f32[832]{0:T(1024)} %copy-done.43) | copy-start | bytes 9988
  733.3 49.8 %copy-start.64 = (bf16[1152,4608]{1,0:T(8,128)(2,1)S(1)}, bf16[1152,4608]{1,0:T(8,128)(2,1)}, u32[]{:S(2)}) copy-start(bf16[1152,4608]{1,0:T(8,128)(2,1)} %all-gather.17.cloned.1.call-done) | copy-start | bytes 31850500
  783.1 14.2 copy-start.36
  798.5 3.7 copy-start.65
  806.3 8.4 copy-start.24
  806.3 8.4 copy-start.28
  806.3 15.8 slice-start
  814.7 7.4 slice-start.1
  822.1 6.2 copy-start.4
  841.8 168.7 %reduce-scatter.10.cloned.1.call-start = ((), (), s32[]{:S(2)}) async-start(), calls=%async_computation.15 | async-start | bytes 10223616 | tf_op jit(solution)/shard_map/reduce_scatter | solution.py:200
  860.6 286.8 %reduce-scatter.16.cloned.1.call-start = ((), (), s32[]{:S(2)}) async-start(), calls=%async_computation.18 | async-start | bytes 3981312 | tf_op jit(solution)/shard_map/reduce_scatter | solution.py:250
  860.6 7.6 copy-start.6
  867.7 283.8 %reduce-scatter.12.cloned.1.call-start = ((), (), s32[]{:S(2)}) async-start(), calls=%async_computation.16 | async-start | bytes 7962624 | tf_op jit(solution)/shard_map/reduce_scatter | solution.py:235
  1040.8 16.8 copy-start.30
  1040.8 16.8 copy-start.38
  1040.8 16.8 copy-start.42
  1057.6 14.3 copy-start.34
  1057.6 14.3 copy-start.11
  1085.0 192.6 %reduce-scatter.18.cloned.1.call-start = ((), (), s32[]{:S(2)}) async-start(), calls=%async_computation.19 | async-start | bytes 15925248 | tf_op jit(solution)/shard_map/reduce_scatter | solution.py:262
  1103.5 300.4 %reduce-scatter.20.cloned.1.call-start = ((), (), s32[]{:S(2)}) async-start(), calls=%async_computation.20 | async-start | bytes 15925248 | tf_op jit(solution)/shard_map/reduce_scatter | solution.py:268
  1131.9 369.4 %reduce-scatter.14.cloned.1.call-start = ((), (), s32[]{:S(2)}) async-start(), calls=%async_computation.17 | async-start | bytes 11943936 | tf_op jit(solution)/shard_map/reduce_scatter | solution.py:247
  1147.3 689.3 %all-reduce.21.cloned.1.call-start = ((), (), s32[]{:S(2)}) async-start(), calls=%async_computation.23 | async-start | bytes 37158912 | tf_op jit(solution)/shard_map/psum | solution.py:290
  1520.2 3.2 copy-start.16
  1534.4 92.6 %all-to-all-start.1 = ((bf16[2,2,239616]{2,1,0:T(2,128)(2,1)}), bf16[2,2,239616]{2,1,0:T(2,128)(2,1)S(1)}, u32[]{:S(2)}, u32[]{:S(2)}) async-start(bf16[2,2,239616]{2,1,0:T(2,128)(2,1)} %reshape.212), calls=%async_computation.3 | async-start | bytes 3833856 | tf_op jit(solution)/shard_map/all_to_all | solution.py:218
  1836.6 4.6 copy-start.23
  1841.2 7.7 slice-start.4
  1844.3 4.7 slice-start.5
  1844.3 10.2 slice-start.2
  1848.9 5.6 slice-start.3
  (26 other events, 46.9 us)
Sparse Core Ops, SparseCore 0:
  9.6 97.7 all-gather.10
  108.9 99.7 all-gather.12
  252.9 86.2 all-gather.20
  341.2 86.2 all-gather.22
  428.9 39.3 all-gather.14
  469.8 130.9 all-gather.16
  602.3 130.9 all-gather.18
  841.9 82.7 reduce-scatter.7
  927.7 82.7 reduce-scatter.9
  1013.1 37.9 reduce-scatter.15
  1085.1 66.3 reduce-scatter.11
  1154.3 123.2 reduce-scatter.17
  1280.6 123.2 reduce-scatter.19
  1406.6 94.6 reduce-scatter.13
  1507.0 329.6 all-reduce.20
where the time goes:
time: 1870 us
  waiting for transfers between devices  1190 us (64%)
  matrix products  253 us (14%)
  local copies, waits for them, and re-layouts  201 us (11%)
  blocking collectives  131 us (7%)
  other arithmetic  62.3 us (3%)
    psum x1, waiting for transfers between devices, per_device(): lax.psum(grad_parts[0].astype(jnp.bfloat16), 'wide').astype(jnp.float32)  191 us
    reduce_scatter x1, waiting for transfers between devices, per_device(): lax.psum_scatter(grad_terms[11].astype(jnp.bfloat16), 'seq', scatter_dime...  126 us
    reduce_scatter x1, waiting for transfers between devices, per_device(): lax.psum_scatter(grad_terms[9].astype(jnp.bfloat16), 'seq', scatter_dimen...  126 us
    all_gather x1, waiting for transfers between devices, per_device(): lax.all_gather(shards[9], 'seq', axis=0, tiled=True)  123 us
    all_gather x1, waiting for transfers between devices, per_device(): lax.all_gather(shards[11], 'seq', axis=0, tiled=True)  115 us
    reduce_scatter x1, waiting for transfers between devices, per_device(): lax.psum_scatter(grad_terms[4].astype(jnp.bfloat16), 'seq', scatter_dimen...  97.4 us
    dot_general x5, matrix products, against(): lax.dot_general(left_side, right_side, (((1,), (1,)), ((), ())), preferre...  91.7 us
    all_gather x1, waiting for transfers between devices, per_device(): lax.all_gather(shards[4], 'seq', axis=0, tiled=True)  89.9 us
  transfers between devices with their start and end apart: 17, of which 14 were waited for; matrix products, arithmetic and copies ran while one was open for 17% of the time, Pallas kernels for 0%

commit v1 on v0

--- a/solution.py
+++ b/solution.py
@@ -287,7 +287,9 @@
         sum_contract,
         sum_contractb,
     ) = (
-        lax.psum(grad_parts[0].astype(jnp.bfloat16), "wide").astype(jnp.float32),
+        jnp.sum(lax.all_gather(grad_parts[0].astype(jnp.bfloat16), "wide"), axis=0).astype(
+            jnp.float32
+        ),
         lax.psum(grad_parts[1].astype(jnp.bfloat16), "wide").astype(jnp.float32),
         lax.psum(grad_parts[2].astype(jnp.bfloat16), "wide").astype(jnp.float32),
         lax.psum(grad_parts[3].astype(jnp.bfloat16), "wide").astype(jnp.float32),

time: 1870 us -> 2000 us (1.070)
  waiting for transfers between devices: 1190 us -> 1310 us
    all_gather x0 -> x1, waiting for transfers between devices: none -> 193 us  [per_device(): lax.all_gather(grad_parts[0].astype(jnp.bfloat16), 'wide')]
    reduce_scatter x1, waiting for transfers between devices: 4.18 us -> 69.2 us  [per_device(): lax.psum_scatter(grad_terms[0].astype(jnp.bfloat16), 'seq', scatter_dimen...]
    reduce_scatter x1, waiting for transfers between devices: 50.4 us -> 1.02 us  [per_device(): lax.psum_scatter(grad_key.astype(jnp.bfloat16), 'seq', scatter_dimension=...]
    reduce_scatter x1, waiting for transfers between devices: 126 us -> 77.2 us  [per_device(): lax.psum_scatter(grad_terms[9].astype(jnp.bfloat16), 'seq', scatter_dimen...]
    psum x1, waiting for transfers between devices: 191 us -> 148 us  [per_device(): lax.psum(grad_parts[4].astype(jnp.bfloat16), 'wide').astype(jnp.float32)]
    unnamed x176 -> x178, local copies, waits for them, and re-layouts: 49.8 us -> 50.4 us
  transfers between devices with their start and end apart: 17 -> 18, of which waited for: 14 -> 15; matrix products, arithmetic and copies ran while one was open for 17% -> 17% of each run, Pallas kernels for 0% -> 0%
where the time goes in v1:
time: 2000 us
  waiting for transfers between devices  1310 us (66%)
  matrix products  252 us (13%)
  local copies, waits for them, and re-layouts  202 us (10%)
  blocking collectives  131 us (7%)
  other arithmetic  76.5 us (4%)
    all_gather x1, waiting for transfers between devices, per_device(): lax.all_gather(grad_parts[0].astype(jnp.bfloat16), 'wide')  193 us
    psum x1, waiting for transfers between devices, per_device(): lax.psum(grad_parts[4].astype(jnp.bfloat16), 'wide').astype(jnp.float32)  148 us
    reduce_scatter x1, waiting for transfers between devices, per_device(): lax.psum_scatter(grad_terms[11].astype(jnp.bfloat16), 'seq', scatter_dime...  126 us
    all_gather x1, waiting for transfers between devices, per_device(): lax.all_gather(shards[9], 'seq', axis=0, tiled=True)  123 us
    all_gather x1, waiting for transfers between devices, per_device(): lax.all_gather(shards[11], 'seq', axis=0, tiled=True)  114 us
    reduce_scatter x1, waiting for transfers between devices, per_device(): lax.psum_scatter(grad_terms[4].astype(jnp.bfloat16), 'seq', scatter_dimen...  97.6 us
    dot_general x5, matrix products, against(): lax.dot_general(left_side, right_side, (((1,), (1,)), ((), ())), preferre...  91.8 us
    all_gather x1, waiting for transfers between devices, per_device(): lax.all_gather(shards[4], 'seq', axis=0, tiled=True)  89.9 us
  transfers between devices with their start and end apart: 18, of which 15 were waited for; matrix products, arithmetic and copies ran while one was open for 17% of the time, Pallas kernels for 0%

profile of v1, /device:TPU:0, one launch (start us, length us, event | category | flops | bytes accessed | tf_op | source)
XLA Modules:
  0.0 1997.3 jit_solution(2964407167140255570)
XLA Ops:
  8.8 5.2 copy.101
  13.9 4.2 all-to-all-start
  21.0 57.0 %all-reduce.18 = (bf16[1152]{0:T(1024)(128)(2,1)S(1)}, bf16[1152]{0:T(1024)(128)(2,1)S(1)}, bf16[1152]{0:T(1024)(128)(2,1)S(1)}, bf16[1152]{0:T(1024)(128)(2,1)S...) all-reduce(bf16[1152]{0:T(1024)(128)(2,1)S(1)} %dynamic-update-slic, ...), channel_id=1, replica_groups=mesh['wide'=16,'seq'=2] {'seq'}, use_global_device_ids=true, to_apply=%add | all-reduce | flops 6912 | bytes 27648
  81.6 4.5 concatenate.9
  86.1 21.3 %all-gather.13.cloned.1.call-done = bf16[2304,1152]{1,0:T(8,128)(2,1)} async-done(((bf16[1152,1152]{1,0:T(8,128)(2,1)}), bf16[2304,1152]{1,0:T(8,128)(2,1)}) %all-gather.13.cloned.1.call-update) | async-done | bytes 5308432 | tf_op jit(solution)/shard_map/all_gather | solution.py:130
  107.4 8.3 fusion.55
  118.8 89.9 %all-gather.15.cloned.1.call-done = bf16[1152,3456]{1,0:T(8,128)(2,1)} async-done(((bf16[576,3456]{1,0:T(8,128)(2,1)}), bf16[1152,3456]{1,0:T(8,128)(2,1)}) %all-gather.15.cloned.1.call-update) | async-done | bytes 7962640 | tf_op jit(solution)/shard_map/all_gather | solution.py:134
  208.8 13.9 convolution_convert_fusion.5
  222.7 21.1 %reshape.156 = bf16[13,64,3,16,72]{4,3,2,1,0:T(8,128)(2,1)} reshape(bf16[832,3456]{1,0:T(8,128)(2,1)} %convolution_convert_fusion.5) | data formatting | bytes 11501568 | tf_op jit(solution)/shard_map/reshape | solution.py:161
  243.8 6.3 fusion.53
  253.1 4.3 copy.125
  260.0 4.4 all-gather.3
  264.6 74.7 %all-gather.23.cloned.1.call-done = bf16[13,128,1,16,72]{4,3,2,0,1:T(8,128)(2,1)} async-done(((bf16[13,64,1,16,72]{4,3,2,0,1:T(8,128)(2,1)}), bf16[13,128,1,16,72]{4,3,2,0,1:T(8,128)(2,1)}) %all-gather.23.cloned.1.call-update) | async-done | bytes 3833872 | tf_op jit(solution)/shard_map/all_gather | solution.py:165
  339.3 9.7 copy.105
  349.0 78.6 %all-gather.25.cloned.1.call-done = bf16[13,128,1,16,72]{4,3,2,0,1:T(8,128)(2,1)} async-done(((bf16[13,64,1,16,72]{4,3,2,0,1:T(8,128)(2,1)}), bf16[13,128,1,16,72]{4,3,2,0,1:T(8,128)(2,1)}) %all-gather.25.cloned.1.call-update) | async-done | bytes 3833872 | tf_op jit(solution)/shard_map/all_gather | solution.py:164
  427.6 9.7 copy.108
  437.2 4.7 fusion.27
  446.5 5.1 convert_bitcast_fusion.1
  454.3 4.7 reshape.157
  459.0 9.4 all-gather.17.cloned.1.call-done
  468.4 6.5 fusion.56
  477.6 123.2 %all-gather.19.cloned.1.call-done = bf16[1152,4608]{1,0:T(8,128)(2,1)} async-done(((bf16[576,4608]{1,0:T(8,128)(2,1)}), bf16[1152,4608]{1,0:T(8,128)(2,1)}) %all-gather.19.cloned.1.call-update) | async-done | bytes 10616848 | tf_op jit(solution)/shard_map/all_gather | solution.py:139
  600.8 18.0 fusion.45
  618.8 114.5 %all-gather.21.cloned.1.call-done = bf16[4608,1152]{1,0:T(8,128)(2,1)} async-done(((bf16[2304,1152]{1,0:T(8,128)(2,1)}), bf16[4608,1152]{1,0:T(8,128)(2,1)}) %all-gather.21.cloned.1.call-update) | async-done | bytes 10616848 | tf_op jit(solution)/shard_map/all_gather | solution.py:141
  733.3 49.8 %fusion.46 = (bf16[4608]{0:T(1024)(128)(2,1)}, bf16[832,4608]{1,0:T(8,128)(2,1)}, f32[832,4608]{1,0:T(8,128)}) fusion(f32[832,4608]{1,0:T(8,128)} %fusion.45, f32[4608]{0:T(1024)S(1)} %reshape.189, bf16[832,1152]{1,0:T(8,128)(2,1)S(1)} %bitcast.95, bf16[4608,1152]{1,0:T(8,128)(2,1)} %all-gather.21.cloned.1.call-done), kind=kOutput, calls=%fused_computation.97 | convolution fusion | flops 9116905472 | bytes 50899968 | tf_op jit(solution)/shard_map/dot_general | solution.py:18
  783.1 14.2 multiply_reduce_fusion.1
  806.3 8.4 reshape.160
  814.7 7.4 multiply_reduce_fusion
  822.1 4.4 multiply_convert_fusion.3
  832.3 9.5 copy.111
  843.8 7.4 convert_bitcast_fusion
  851.2 9.5 copy.114
  862.4 6.2 convolution_convert_fusion.4
  868.7 18.4 convolution_convert_fusion.1
  887.2 11.1 multiply_convert_fusion
  901.3 14.5 convolution_convert_fusion
  917.8 6.0 fusion.22
  927.7 82.3 %reduce-scatter.10.cloned.1.call-done = bf16[13,64,16,72]{3,2,0,1:T(8,128)(2,1)} async-done(((bf16[13,128,16,72]{3,2,0,1:T(8,128)(2,1)}), bf16[13,64,16,72]{3,2,0,1:T(8,128)(2,1)}) %reduce-scatter.10.cloned.1.call-update) | async-done | bytes 1916944 | tf_op jit(solution)/shard_map/reduce_scatter | solution.py:200
  1010.0 4.7 copy.141
  1014.7 9.3 pad_maximum_fusion
  1024.0 16.0 copy.116
  1040.0 16.8 convert_element_type.216
  1056.8 14.6 convolution_convert_fusion.2
  1072.0 14.5 multiply_reduce_fusion.2
  1091.5 8.0 convolution_convert_fusion.3
  1099.6 77.2 %reduce-scatter.18.cloned.1.call-done = bf16[576,4608]{1,0:T(8,128)(2,1)} async-done(((bf16[1152,4608]{1,0:T(8,128)(2,1)}), bf16[576,4608]{1,0:T(8,128)(2,1)}) %reduce-scatter.18.cloned.1.call-update) | async-done | bytes 5308432 | tf_op jit(solution)/shard_map/reduce_scatter | solution.py:262
  1176.8 126.1 %reduce-scatter.20.cloned.1.call-done = bf16[2304,1152]{1,0:T(8,128)(2,1)} async-done(((bf16[4608,1152]{1,0:T(8,128)(2,1)}), bf16[2304,1152]{1,0:T(8,128)(2,1)}) %reduce-scatter.20.cloned.1.call-update) | async-done | bytes 5308432 | tf_op jit(solution)/shard_map/reduce_scatter | solution.py:268
  1303.0 97.6 %reduce-scatter.14.cloned.1.call-done = bf16[576,3456]{1,0:T(8,128)(2,1)} async-done(((bf16[1152,3456]{1,0:T(8,128)(2,1)}), bf16[576,3456]{1,0:T(8,128)(2,1)}) %reduce-scatter.14.cloned.1.call-update) | async-done | bytes 3981328 | tf_op jit(solution)/shard_map/reduce_scatter | solution.py:247
  1400.7 69.2 %reduce-scatter.12.cloned.1.call-done = bf16[1152,1152]{1,0:T(8,128)(2,1)} async-done(((bf16[2304,1152]{1,0:T(8,128)(2,1)}), bf16[1152,1152]{1,0:T(8,128)(2,1)}) %reduce-scatter.12.cloned.1.call-update) | async-done | bytes 2654224 | tf_op jit(solution)/shard_map/reduce_scatter | solution.py:235
  1471.8 7.6 all-reduce.17
  1479.5 9.2 fusion.57
  1492.0 5.5 copy.117
  1497.6 5.4 reshape.213
  1506.7 17.1 fusion.19
  1523.8 4.3 slice.24
  1528.7 62.0 %all-reduce.15 = (bf16[576]{0:T(1024)(128)(2,1)S(1)}, bf16[576]{0:T(1024)(128)(2,1)S(1)}, bf16[576]{0:T(1024)(128)(2,1)S(1)}, bf16[576]{0:T(1024)(128)(2,1)S(1)}...) all-reduce(bf16[576]{0:T(1024)(128)(2,1)S(1)} %dynamic-slice.8, ...), channel_id=1, replica_groups=mesh['wide'=16,'seq'=2] {'wide'}, use_global_device_ids=true, to_apply=%region_17.18 | all-reduce | flops 6336 | bytes 25344 | tf_op jit(solution)/shard_map/psum | solution.py:293
  1595.5 4.4 reshape.214
  1599.8 9.1 copy.122
  1613.7 148.1 %all-reduce.21.cloned.1.call-done = (bf16[576,3456]{1,0:T(8,128)(2,1)}, bf16[576,1152]{1,0:T(8,128)(2,1)}, bf16[576,4608]{1,0:T(8,128)(2,1)}, bf16[2304,1152]{1,0:T(8,128)(2,1)}) async-done(((bf16[576,3456]{1,0:T(8,128)(2,1)}, bf16[576,1152]{1,0:T(8,128)(2,1)}, bf16[576,4608]{1,0:T(8,128)(2,1)}, bf16[2304,1152]{1,0:T(8,128)(2,1)}), (bf16[576,3456]{1,0:T(8,128)(2,1)}, bf16[576,1152]{1,0:T(8,128)(2,1)}, ...) | async-done | bytes 15925264 | tf_op jit(solution)/shard_map/psum | solution.py:296
  1765.0 4.7 convert_element_type.226
  1769.7 5.6 convert_element_type.235
  1775.3 4.8 convert_element_type.238
  1780.1 193.4 %all-gather.27.cloned.1.call-done = bf16[18432,1152]{1,0:T(8,128)(2,1)} async-done(((bf16[1152,1152]{1,0:T(8,128)(2,1)}), bf16[18432,1152]{1,0:T(8,128)(2,1)}) %all-gather.27.cloned.1.call-update) | async-done | bytes 42467344 | tf_op jit(solution)/shard_map/all_gather | solution.py:290
  1973.5 14.3 reduce_sum.210
  (258 shorter events, 82.5 us)
Async XLA Ops:
  7.2 100.2 %all-gather.13.cloned.1.call-start = ((), (), s32[]{:S(2)}) async-start(), calls=%async_computation.9 | async-start | bytes 7962624 | tf_op jit(solution)/shard_map/all_gather | solution.py:130
  7.9 200.8 %all-gather.15.cloned.1.call-start = ((), (), s32[]{:S(2)}) async-start(), calls=%async_computation.10 | async-start | bytes 11943936 | tf_op jit(solution)/shard_map/all_gather | solution.py:134
  8.7 9.5 copy-start.56
  8.7 10.8 copy-start.57
  8.7 11.0 copy-start.58
  8.7 11.3 copy-start.59
  8.7 11.5 copy-start.60
  8.7 11.7 copy-start.61
  8.7 12.0 copy-start.62
  13.9 64.1 %all-to-all-start = ((bf16[13,128,576]{2,0,1:T(8,128)(2,1)}), bf16[13,128,576]{2,0,1:T(8,128)(2,1)S(1)}, u32[]{:S(2)}, u32[]{:S(2)}) async-start(bf16[13,128,576]{2,0,1:T(8,128)(2,1)} %copy.101), calls=%async_computation | async-start | bytes 5242880 | tf_op jit(solution)/shard_map/all_to_all | solution.py:156
  18.2 321.1 %all-gather.23.cloned.1.call-start = ((), (), s32[]{:S(2)}) async-start(), calls=%async_computation.21 | async-start | bytes 10223616 | tf_op jit(solution)/shard_map/all_gather | solution.py:165
  78.0 130.8 %copy-start.38 = (f32[1152]{0:T(1024)}, f32[1152]{0:T(1024)S(1)}, u32[]{:S(2)}) copy-start(f32[1152]{0:T(1024)S(1)} %convert_element_type.191) | copy-start | bytes 13828
  78.0 130.8 %copy-start.49 = (f32[1152]{0:T(1024)}, f32[1152]{0:T(1024)S(1)}, u32[]{:S(2)}) copy-start(f32[1152]{0:T(1024)S(1)} %convert_element_type.192) | copy-start | bytes 13828
  86.1 29.6 %copy-start.22 = (bf16[832,1152]{1,0:T(8,128)(2,1)}, bf16[832,1152]{1,0:T(8,128)(2,1)S(1)}, u32[]{:S(2)}) copy-start(bf16[832,1152]{1,0:T(8,128)(2,1)S(1)} %concatenate.9) | copy-start | bytes 5750788
  115.7 106.9 %copy-start.30 = (f32[832]{0:T(1024)}, f32[832]{0:T(1024)S(1)}, u32[]{:S(2)}) copy-start(f32[832]{0:T(1024)S(1)} %broadcast_multiply_fusion.1) | copy-start | bytes 9988
  118.8 103.8 %copy-start.42 = (f32[832]{0:T(1024)}, f32[832]{0:T(1024)S(1)}, u32[]{:S(2)}) copy-start(f32[832]{0:T(1024)S(1)} %fusion.37) | copy-start | bytes 9988
  250.1 187.1 %copy-start.3 = (bf16[13,64,1,16,72]{4,3,2,1,0:T(8,128)(2,1)}, bf16[13,64,1,16,72]{4,3,2,1,0:T(8,128)(2,1)S(1)}, u32[]{:S(2)}) copy-start(bf16[13,64,1,16,72]{4,3,2,1,0:T(8,128)(2,1)S(1)} %get-tuple-element.142) | copy-start | bytes 5750788
  252.8 174.7 %all-gather.25.cloned.1.call-start = ((), (), s32[]{:S(2)}) async-start(), calls=%async_computation.22 | async-start | bytes 10223616 | tf_op jit(solution)/shard_map/all_gather | solution.py:164
  257.4 211.0 %all-gather.17.cloned.1.call-start = ((), (), s32[]{:S(2)}) async-start(), calls=%async_computation.11 | async-start | bytes 3981312 | tf_op jit(solution)/shard_map/all_gather | solution.py:135
  258.0 342.8 %all-gather.19.cloned.1.call-start = ((), (), s32[]{:S(2)}) async-start(), calls=%async_computation.12 | async-start | bytes 15925248 | tf_op jit(solution)/shard_map/all_gather | solution.py:139
  258.6 474.7 %all-gather.21.cloned.1.call-start = ((), (), s32[]{:S(2)}) async-start(), calls=%async_computation.13 | async-start | bytes 15925248 | tf_op jit(solution)/shard_map/all_gather | solution.py:141
  259.3 665.4 %reduce-scatter.8.cloned.1.call-start = ((), (), s32[]{:S(2)}) async-start(), calls=%async_computation.14 | async-start | bytes 10223616 | tf_op jit(solution)/shard_map/reduce_scatter | solution.py:197
  259.4 341.4 %copy-start.40 = (f32[1152]{0:T(1024)}, f32[1152]{0:T(1024)S(1)}, u32[]{:S(2)}) copy-start(f32[1152]{0:T(1024)S(1)} %convert_element_type.199) | copy-start | bytes 13828
  259.4 341.4 %copy-start.51 = (f32[1152]{0:T(1024)}, f32[1152]{0:T(1024)S(1)}, u32[]{:S(2)}) copy-start(f32[1152]{0:T(1024)S(1)} %convert_element_type.200) | copy-start | bytes 13828
  264.6 181.4 %copy-start.28 = (pred[13,128]{1,0:T(8,128)(4,1)}, pred[13,128]{1,0:T(8,128)(4,1)S(1)}, u32[]{:S(2)}) copy-start(pred[13,128]{1,0:T(8,128)(4,1)S(1)} %iota_compare_fusion) | copy-start | bytes 4996
  441.9 9.7 copy-start
  474.9 143.9 %copy-start.32 = (f32[832]{0:T(1024)}, f32[832]{0:T(1024)S(1)}, u32[]{:S(2)}) copy-start(f32[832]{0:T(1024)S(1)} %broadcast_multiply_fusion) | copy-start | bytes 9988
  477.0 141.9 %copy-start.44 = (f32[832]{0:T(1024)}, f32[832]{0:T(1024)S(1)}, u32[]{:S(2)}) copy-start(f32[832]{0:T(1024)S(1)} %fusion.38) | copy-start | bytes 9988
  477.6 255.7 %copy-start.7 = (bf16[13,64,1152]{2,1,0:T(8,128)(2,1)S(1)}, bf16[13,64,1152]{2,1,0:T(8,128)(2,1)}, u32[]{:S(2)}) copy-start(bf16[13,64,1152]{2,1,0:T(8,128)(2,1)} %param.20) | copy-start | bytes 5750788
  733.3 49.8 %copy-start.12 = (f32[832,1152]{1,0:T(8,128)S(1)}, f32[832,1152]{1,0:T(8,128)}, u32[]{:S(2)}) copy-start(f32[832,1152]{1,0:T(8,128)} %copy-done.11) | copy-start | bytes 11501572
  733.3 49.8 %copy-start.33 = (f32[832]{0:T(1024)S(1)}, f32[832]{0:T(1024)}, u32[]{:S(2)}) copy-start(f32[832]{0:T(1024)} %copy-done.32) | copy-start | bytes 9988
  733.3 49.8 %copy-start.41 = (f32[1152]{0:T(1024)S(1)}, f32[1152]{0:T(1024)}, u32[]{:S(2)}) copy-start(f32[1152]{0:T(1024)} %copy-done.40) | copy-start | bytes 13828
  733.3 49.8 %copy-start.45 = (f32[832]{0:T(1024)S(1)}, f32[832]{0:T(1024)}, u32[]{:S(2)}) copy-start(f32[832]{0:T(1024)} %copy-done.44) | copy-start | bytes 9988
  733.3 49.8 %copy-start.65 = (bf16[1152,4608]{1,0:T(8,128)(2,1)S(1)}, bf16[1152,4608]{1,0:T(8,128)(2,1)}, u32[]{:S(2)}) copy-start(bf16[1152,4608]{1,0:T(8,128)(2,1)} %all-gather.19.cloned.1.call-done) | copy-start | bytes 31850500
  783.1 14.3 copy-start.37
  806.3 8.4 copy-start.25
  806.3 8.4 copy-start.29
  806.3 15.8 slice-start
  814.6 7.4 slice-start.1
  841.9 168.1 %reduce-scatter.10.cloned.1.call-start = ((), (), s32[]{:S(2)}) async-start(), calls=%async_computation.15 | async-start | bytes 10223616 | tf_op jit(solution)/shard_map/reduce_scatter | solution.py:200
  860.8 7.9 copy-start.46
  860.8 7.9 copy-start.52
  860.8 238.8 %reduce-scatter.16.cloned.1.call-start = ((), (), s32[]{:S(2)}) async-start(), calls=%async_computation.18 | async-start | bytes 3981312 | tf_op jit(solution)/shard_map/reduce_scatter | solution.py:250
  868.7 308.2 %reduce-scatter.18.cloned.1.call-start = ((), (), s32[]{:S(2)}) async-start(), calls=%async_computation.19 | async-start | bytes 15925248 | tf_op jit(solution)/shard_map/reduce_scatter | solution.py:262
  887.1 415.9 %reduce-scatter.20.cloned.1.call-start = ((), (), s32[]{:S(2)}) async-start(), calls=%async_computation.20 | async-start | bytes 15925248 | tf_op jit(solution)/shard_map/reduce_scatter | solution.py:268
  887.2 14.1 copy-start.8
  915.8 484.7 %reduce-scatter.14.cloned.1.call-start = ((), (), s32[]{:S(2)}) async-start(), calls=%async_computation.17 | async-start | bytes 11943936 | tf_op jit(solution)/shard_map/reduce_scatter | solution.py:247
  1040.0 16.8 copy-start.31
  1040.0 16.8 copy-start.39
  1040.0 16.8 copy-start.43
  1040.0 16.8 copy-start.50
  1071.5 15.0 copy-start.35
  1071.5 398.4 %reduce-scatter.12.cloned.1.call-start = ((), (), s32[]{:S(2)}) async-start(), calls=%async_computation.16 | async-start | bytes 7962624 | tf_op jit(solution)/shard_map/reduce_scatter | solution.py:235
  1071.9 14.6 copy-start.14
  1099.6 662.2 %all-reduce.21.cloned.1.call-start = ((), (), s32[]{:S(2)}) async-start(), calls=%async_computation.24 | async-start | bytes 31850496 | tf_op jit(solution)/shard_map/psum | solution.py:296
  1400.6 71.0 %copy-start.63 = (bf16[576]{0:T(1024)(128)(2,1)S(1)}, bf16[576]{0:T(1024)(128)(2,1)}, u32[]{:S(2)}) copy-start(bf16[576]{0:T(1024)(128)(2,1)} %param.33) | copy-start | bytes 3460
  1400.6 71.2 %copy-start.47 = (bf16[1152]{0:T(1024)(128)(2,1)S(1)}, bf16[1152]{0:T(1024)(128)(2,1)}, u32[]{:S(2)}) copy-start(bf16[1152]{0:T(1024)(128)(2,1)} %get-tuple-element.132) | copy-start | bytes 6916
  1400.6 71.2 %copy-start.48 = (bf16[4608]{0:T(1024)(128)(2,1)S(1)}, bf16[4608]{0:T(1024)(128)(2,1)}, u32[]{:S(2)}) copy-start(bf16[4608]{0:T(1024)(128)(2,1)} %get-tuple-element.129) | copy-start | bytes 27652
  1400.6 71.2 %copy-start.54 = (bf16[1152]{0:T(1024)(128)(2,1)S(1)}, bf16[1152]{0:T(1024)(128)(2,1)}, u32[]{:S(2)}) copy-start(bf16[1152]{0:T(1024)(128)(2,1)} %get-tuple-element.96) | copy-start | bytes 6916
  1400.6 71.2 %copy-start.55 = (bf16[1152]{0:T(1024)(128)(2,1)S(1)}, bf16[1152]{0:T(1024)(128)(2,1)}, u32[]{:S(2)}) copy-start(bf16[1152]{0:T(1024)(128)(2,1)} %get-tuple-element.100) | copy-start | bytes 6916
  1400.6 572.8 %all-gather.27.cloned.1.call-start = ((), (), s32[]{:S(2)}) async-start(), calls=%async_computation.23 | async-start | bytes 45121536 | tf_op jit(solution)/shard_map/all_gather | solution.py:290
  1502.9 92.5 %all-to-all-start.1 = ((bf16[2,2,239616]{2,1,0:T(2,128)(2,1)}), bf16[2,2,239616]{2,1,0:T(2,128)(2,1)S(1)}, u32[]{:S(2)}, u32[]{:S(2)}) async-start(bf16[2,2,239616]{2,1,0:T(2,128)(2,1)} %reshape.213), calls=%async_computation.3 | async-start | bytes 3833856 | tf_op jit(solution)/shard_map/all_to_all | solution.py:218
  1761.8 7.9 slice-start.4
  1765.0 10.3 slice-start.2
  (28 other events, 77.4 us)
Sparse Core Ops, SparseCore 0:
  9.6 97.7 all-gather.12
  108.9 99.7 all-gather.14
  252.9 86.2 all-gather.22
  341.2 86.2 all-gather.24
  428.9 39.3 all-gather.16
  469.8 130.9 all-gather.18
  602.3 130.9 all-gather.20
  842.0 82.7 reduce-scatter.7
  927.2 82.7 reduce-scatter.9
  1012.7 37.9 reduce-scatter.15
  1053.5 123.2 reduce-scatter.17
  1179.7 123.2 reduce-scatter.19
  1305.9 94.6 reduce-scatter.13
  1403.4 66.4 reduce-scatter.11
  1475.0 286.8 all-reduce.20
  1763.3 210.0 all-gather.26
